TPU v7x, 256 devices: a whole 4x4x8 slice. The times are simulated.
256 devices in a mesh: tm: 8 (over y, core), rows: 32 (over z, x).
Axes of the slice: x: 4, y: 4, z: 8, core: 2. Of those that a mesh axis runs over, the one named last changes fastest.
Arguments:
- features: bfloat16 [32, 64, 320, 128], P('tm', 'rows'), may hold values from -20 to 20
- gain_one: float32 [128], replicated, may hold values from 0.1 to 1.9
- shift_one: float32 [128], replicated, may hold values from -4 to 4
- weight_one: bfloat16 [3456, 128], replicated, may hold values from -0.109375 to 0.109375
- bias_one: float32 [128], replicated, may hold values from -6 to 6
- gain_two: float32 [128], replicated, may hold values from 0.1 to 1.9
- shift_two: float32 [128], replicated, may hold values from -4 to 4
- weight_two: bfloat16 [3456, 128], replicated, may hold values from -0.109375 to 0.109375
- bias_two: float32 [128], replicated, may hold values from -6 to 6
Outputs:
- block_out: bfloat16 [32, 64, 320, 128], P('tm', 'rows')
All inputs are finite; a program needn't handle non-finite values.
Results may differ from a plain program's by a relative error of at most 0.007.
Values may be sent and summed in bfloat16 or wider, within the bound.
No kernel may reach another device: no remote copies, remote signals or barrier semaphores. Data moves between devices by JAX's collectives and lax.ppermute only.
A program may use at most 64 MiB of HBM per device.

v0:
```python
import functools

import jax
import jax.numpy as jnp
from jax import lax
from jax.experimental import pallas as pl
from jax.experimental.pallas import tpu as pltpu
from jax.sharding import Mesh
from jax.sharding import PartitionSpec as P

C = 128
GROUP = 4
TM = ("y", "c")
ROWS = ("z", "x")
EVERY = TM + ROWS
STAGES_ONE = (("y", "c", "z"), ("x",))
STAGES_TWO = (("y", "z"), ("c", "x"))
EPS = 1e-06
MIB = 1 << 20
VMEM = pl.BlockSpec(memory_space=pltpu.VMEM)
HBM = pl.BlockSpec(memory_space=pltpu.HBM)


def group_total(v):
    lane = lax.broadcasted_iota(jnp.int32, v.shape, v.ndim - 1)
    for step in (1, 2):
        ahead = pltpu.roll(v, C - step, v.ndim - 1)
        behind = pltpu.roll(v, step, v.ndim - 1)
        v = v + jnp.where((lane & step) == 0, ahead, behind)
    return v


def lane_place(shape):
    return lax.broadcasted_iota(jnp.int32, shape, len(shape) - 1) % GROUP


def packed(first, centered):
    place = lane_place(first.shape)
    return jnp.where(place == 0, first, jnp.where(place == 1, centered, 0.0))


def column_total(rows):
    total = rows if rows.shape[0] < 8 else jnp.sum(rows.reshape(rows.shape[0] // 8, 8, C), axis=0)
    return jnp.broadcast_to(jnp.sum(total, axis=0, keepdims=True), (8, C))


def merged(every, cells):
    count = every.shape[0]
    total = column_total(every)
    place = lane_place(total.shape)
    first = group_total(jnp.where(place == 0, total, 0.0))
    apart = every / cells - first[:1] / (cells * count)
    between = column_total(apart * apart) * cells
    centered = group_total(jnp.where(place == 0, between, jnp.where(place == 1, total, 0.0)))
    return first, centered


def scale_and_offset(sums_ref, vectors_ref, which, tile_cells, devices):
    count = sums_ref.shape[0]
    cells = tile_cells * GROUP * devices
    first, centered = merged(sums_ref[...], cells // count)
    average, spread = first[:1] / cells, centered[:1] / cells
    scale = lax.rsqrt(spread + EPS) * vectors_ref[which : which + 1]
    offset = vectors_ref[which + 1 : which + 2] - average * scale
    return 0.5 * scale, 0.5 * offset


def activated(values, scale, offset):
    half = values.astype(jnp.float32) * scale + offset
    return (half + half * jnp.tanh(half)).astype(jnp.bfloat16)


def taps(act_ref, w_ref, f, wraps):
    width = act_ref.shape[2]
    column = lax.broadcasted_iota(jnp.int32, (width, C), 0)

    def left(rows, unused):
        pieces = []
        for i in range(3):
            for r in rows:
                piece = act_ref[f + i, r]
                if wraps is not None and r == unused:
                    piece = jnp.where(wraps, jnp.zeros_like(piece), piece)
                pieces.append(piece)
        return jnp.concatenate(pieces, axis=1)

    def block(i, j, k):
        if not 0 <= j < 3:
            return jnp.zeros((C, C), jnp.bfloat16)
        first = ((i * 3 + j) * 3 + k) * C
        return w_ref[first : first + C, :]

    def pair(i, r, out, k):
        found = block(i, r - out, k)
        if wraps is not None and 0 <= r - out < 3 and r // 2 != out:
            found = jnp.where(wraps, jnp.zeros_like(found), found)
        return found

    early = jnp.concatenate(
        [jnp.concatenate([block(i, j, 0), block(i, j, 1)], axis=1) for i in range(3) for j in range(3)],
        axis=0,
    )
    late = jnp.concatenate(
        [jnp.concatenate([pair(i, r, 0, 2), pair(i, r, 1, 2)], axis=1) for i in range(3) for r in range(4)],
        axis=0,
    )
    ends = jnp.dot(left(range(4), None), late, preferred_element_type=jnp.float32)
    totals = []
    for out in range(2):
        part = jnp.dot(left(range(out, out + 3), 2 - out), early, preferred_element_type=jnp.float32)
        before = jnp.where(column == 0, 0.0, pltpu.roll(part[:, :C], 1, 0))
        after = ends[:, out * C : (out + 1) * C]
        after = jnp.where(column == width - 1, 0.0, pltpu.roll(after, width - 1, 0))
        totals.append(before + part[:, C:] + after)
    return totals


def conv(sources, act_ref, w_ref, wraps, emit, ready=None):
    earlier = 2
    frames, rows = act_ref.shape[0], act_ref.shape[1]

    def fill(f):
        for r in range(rows):
            act_ref[f, r] = sources(f, r)

    for f in range(earlier + 2):
        fill(f)
    if ready is not None:
        ready()
    for f in range(frames - earlier):
        if f > 1:
            fill(f + earlier)
        emit(f, taps(act_ref, w_ref, f, wraps))


def source_of(own_ref, rows_ref, back_ref, diagonal_ref, own_low, back_low, tm, scale, offset, hides):
    earlier = back_ref.shape[0]

    def pick(low, one, other, r):
        return jnp.where(low if r < 2 else jnp.logical_not(low), one, other)

    def sources(f, r):
        here = max(f - earlier, 0)
        value = pick(own_low, own_ref[here, r % 2], rows_ref[here, r % 2], r)
        if f < earlier:
            past = pick(back_low, back_ref[f, r % 2], diagonal_ref[f, r % 2], r)
            value = jnp.where(tm == 0, value, past)
        value = activated(value, scale, offset)
        if r in hides:
            value = jnp.where(hides[r], jnp.zeros_like(value), value)
        return value

    return sources


class Sums:
    def __init__(self, rows, width):
        self.cells, self.width = rows * width, width
        self.center, self.firsts, self.squares = None, [], []

    def folded(self, values):
        return sum(v.reshape(self.width // 8, 8, C).sum(axis=0) for v in values)

    def add(self, values):
        if self.center is None:
            self.center = jnp.sum(self.folded(values), axis=0, keepdims=True) / self.cells
        apart = [v - self.center for v in values]
        self.firsts.append(self.folded(apart))
        self.squares.append(self.folded([v * v for v in apart]))

    def both(self):
        cells = self.cells * len(self.firsts)
        first = jnp.sum(sum(self.firsts), axis=0, keepdims=True)
        square = jnp.sum(sum(self.squares), axis=0, keepdims=True)
        mean = self.center + first / cells
        whole = group_total(jnp.broadcast_to(mean * cells, (8, C)))
        apart = mean - whole[:1] / (cells * GROUP)
        centered = square - first * first / cells + cells * apart * apart
        return packed(whole, group_total(jnp.broadcast_to(centered, (8, C))))


def moments_kernel(x_hbm, *refs):
    vectors_hbm, (last_ref, sums_ref, vectors_ref, x_ref, x_sems, vector_sems) = refs[:-6], refs[-6:]
    frames, rows, width, _ = x_ref.shape
    earlier = last_ref.shape[0]
    copies = [pltpu.make_async_copy(x_hbm.at[f], x_ref.at[f], x_sems.at[f]) for f in range(frames)]
    small = [
        pltpu.make_async_copy(v, vectors_ref.at[i : i + 1], vector_sems.at[i])
        for i, v in enumerate(vectors_hbm)
    ]
    for copy in copies + small:
        copy.start()
    sums = Sums(rows, width)
    for f in range(frames):
        copies[f].wait()
        sums.add([x_ref[f, r].astype(jnp.float32) for r in range(rows)])
        if f >= frames - earlier:
            last_ref[f - frames + earlier] = x_ref[f]
    sums_ref[...] = jnp.broadcast_to(sums.both()[:1], sums_ref.shape)
    for copy in small:
        copy.wait()


def relay_kernel(cells, sums_ref, next_ref):
    both = packed(*merged(sums_ref[...], cells))
    next_ref[...] = jnp.broadcast_to(both[:1], next_ref.shape)


def first_conv_kernel(
    devices, last_row, own_ref, rows_ref, back_ref, diagonal_ref, sums_ref, vectors_ref, w_hbm,
    hidden_ref, last_ref, next_ref, act_ref, w_ref, w_sem,
):
    weights = pltpu.make_async_copy(w_hbm, w_ref, w_sem)
    weights.start()
    frames, rows, width, _ = own_ref.shape
    earlier = back_ref.shape[0]
    core, tm, row = lax.axis_index("c"), lax.axis_index(TM), lax.axis_index(ROWS)
    scale, offset = scale_and_offset(sums_ref, vectors_ref, 0, frames * rows * width, devices)
    low = core == 1
    sources = source_of(own_ref, rows_ref, back_ref, diagonal_ref, low, low, tm, scale, offset, {})
    sums = Sums(rows, width)

    def emit(f, totals):
        rounded = [(v + vectors_ref[2:3]).astype(jnp.bfloat16) for v in totals]
        for r, v in enumerate(rounded):
            hidden_ref[f, r] = v
            if f >= frames - earlier:
                last_ref[f - frames + earlier, r] = v
        sums.add([v.astype(jnp.float32) for v in rounded])

    conv(sources, act_ref, w_ref, row == core * last_row, emit, weights.wait)
    next_ref[...] = jnp.broadcast_to(sums.both()[:1], next_ref.shape)


def second_conv_kernel(
    devices, last_row, own_ref, rows_ref, back_ref, diagonal_ref, sums_ref, vectors_ref, w_hbm,
    features_hbm, out_hbm, act_ref, w_ref, w_sem, features_ref, sem, out_ref, out_sems,
):
    weights = pltpu.make_async_copy(w_hbm, w_ref, w_sem)
    weights.start()
    residual = pltpu.make_async_copy(features_hbm, features_ref, sem)
    residual.start()
    frames, rows, width, _ = own_ref.shape
    core, tm, row = lax.axis_index("c"), lax.axis_index(TM), lax.axis_index(ROWS)
    scale, offset = scale_and_offset(sums_ref, vectors_ref, 3, frames * rows * width, devices)
    hides = {0: row == 0, act_ref.shape[1] - 1: row == last_row}
    sources = source_of(
        own_ref, rows_ref, back_ref, diagonal_ref, core == 0, core == 1, tm, scale, offset, hides
    )

    def emit(f, totals):
        for r, v in enumerate(totals):
            value = v + vectors_ref[5:6] + features_ref[f, r].astype(jnp.float32)
            out_ref[f, r] = value.astype(jnp.bfloat16)
        outs[f].start()

    outs = [pltpu.make_async_copy(out_ref.at[f], out_hbm.at[f], out_sems.at[f]) for f in range(frames)]

    def ready():
        weights.wait()
        residual.wait()

    conv(sources, act_ref, w_ref, None, emit, ready)
    for copy in outs:
        copy.wait()


def sent(block, tm_step, row_steps):
    tms, rows = lax.axis_size(TM), lax.axis_size(ROWS)
    route = []
    for t in range(tms):
        for r in range(rows):
            source = (t - tm_step, (r + row_steps[t % 2]) % rows)
            if source[0] >= 0:
                route.append((source[0] * rows + source[1], t * rows + r))
    return lax.ppermute(block, EVERY, route)


def neighbours(own, last, row_steps):
    beside = sent(own, 0, row_steps)
    back = sent(last, 1, (0, 0))
    diagonal = sent(last, 1, (-1, 1))
    return beside, back, diagonal


def in_hbm(array):
    return pltpu.with_memory_space_constraint(array, pltpu.HBM)


def exchanged(copies, axes):
    count = copies.shape[0]
    received = lax.all_to_all(copies.reshape(count, 1, C), axes, split_axis=0, concat_axis=0, tiled=True)
    return received.reshape(count, C)


def everywhere(copies, tile_cells, stages):
    far, near = stages
    sums = exchanged(copies, far)
    copies = pl.pallas_call(
        functools.partial(relay_kernel, tile_cells * GROUP),
        out_shape=jax.ShapeDtypeStruct((lax.axis_size(near), C), jnp.float32),
        in_specs=[VMEM],
        out_specs=VMEM,
        name="relay",
        cost_estimate=pl.CostEstimate(flops=0, bytes_accessed=1 << 24, transcendentals=0),
        compiler_params=pltpu.CompilerParams(vmem_limit_bytes=4 * MIB),
    )(sums)
    return exchanged(copies, near)


def body(features, gain_one, shift_one, weight_one, bias_one, gain_two, shift_two, weight_two, bias_two):
    frames, rows, width, _ = features.shape
    devices = lax.axis_size(EVERY)
    tile_cells = frames * rows * width
    copies_one, copies_two = (
        jax.ShapeDtypeStruct((lax.axis_size(stages[0]), C), jnp.float32) for stages in (STAGES_ONE, STAGES_TWO)
    )
    tile = jax.ShapeDtypeStruct(features.shape, jnp.bfloat16)
    two = jax.ShapeDtypeStruct((2, rows, width, C), jnp.bfloat16)
    last_row = lax.axis_size(ROWS) - 1
    held = pltpu.VMEM((frames + 2, rows + 2, width, C), jnp.bfloat16)
    limit = pltpu.CompilerParams(vmem_limit_bytes=10 * MIB)
    vectors = [v.reshape(1, C) for v in (gain_one, shift_one, bias_one, gain_two, shift_two, bias_two)]

    last, sums, vectors = pl.pallas_call(
        moments_kernel,
        out_shape=(two, copies_one, jax.ShapeDtypeStruct((8, C), jnp.float32)),
        in_specs=[HBM] * 7,
        out_specs=(VMEM,) * 3,
        scratch_shapes=[
            pltpu.VMEM(features.shape, jnp.bfloat16),
            pltpu.SemaphoreType.DMA((frames,)),
            pltpu.SemaphoreType.DMA((len(vectors),)),
        ],
        name="moments",
        compiler_params=pltpu.CompilerParams(vmem_limit_bytes=4 * MIB),
    )(*(in_hbm(v) for v in (features, *vectors)))
    around = neighbours(features, last, (-1, 1))
    sums = everywhere(sums, tile_cells, STAGES_ONE)
    hidden, last, sums_two = pl.pallas_call(
        functools.partial(first_conv_kernel, devices, last_row),
        out_shape=(tile, two, copies_two),
        in_specs=[VMEM] * 6 + [HBM],
        out_specs=(VMEM,) * 3,
        scratch_shapes=[held, pltpu.VMEM(weight_one.shape, weight_one.dtype), pltpu.SemaphoreType.DMA],
        name="first_conv",
        compiler_params=limit,
    )(features, *around, sums, vectors, in_hbm(weight_one))

    around = neighbours(hidden, last, (1, -1))
    sums_two = everywhere(sums_two, tile_cells, STAGES_TWO)
    return pl.pallas_call(
        functools.partial(second_conv_kernel, devices, last_row),
        out_shape=tile,
        in_specs=[VMEM] * 6 + [HBM] * 2,
        out_specs=HBM,
        scratch_shapes=[
            held,
            pltpu.VMEM(weight_two.shape, weight_two.dtype),
            pltpu.SemaphoreType.DMA,
            pltpu.VMEM(features.shape, features.dtype),
            pltpu.SemaphoreType.DMA,
            pltpu.VMEM(features.shape, features.dtype),
            pltpu.SemaphoreType.DMA((frames,)),
        ],
        name="second_conv",
        compiler_params=limit,
    )(hidden, *around, sums_two, vectors, in_hbm(weight_two), in_hbm(features))


def solution(mesh):
    split = Mesh(mesh.devices.reshape(4, 2, 8, 4), EVERY)
    return jax.shard_map(
        body,
        mesh=split,
        in_specs=(P(TM, ROWS, None, None), P(), P(), P(), P(), P(), P(), P(), P()),
        out_specs=P(TM, ROWS, None, None),
        check_vma=False,
    )
```

profile of v0, /device:TPU:1, one launch (start us, length us, event | category | flops | bytes accessed | tf_op | source)
XLA Modules:
  0.0 80.7 jit_solution(11015091181144794989)
XLA Ops:
  0.0 0.0 copy-start
  0.0 8.6 %collective-permute-start = (bf16[4,2,320,128]{3,2,1,0:T(8,128)(2,1)}, bf16[4,2,320,128]{3,2,1,0:T(8,128)(2,1)S(1)}, u32[]{:S(2)}, u32[]{:S(2)}) collective-permute-start(bf16[4,2,320,128]{3,2,1,0:T(8,128)(2,1)} %features_hbm.1), channel_id=1, source_target_pairs={{31,0},{0,1},{1,2},{2,3},{3,4},{4,5},{5,6},{6,7},{7,8},{8,9},{9,10... | collective-permute-start | bytes 1966088 | tf_op jit(solution)/shard_map/ppermute | solution.py:276
  8.6 1.7 %moments.1 = (bf16[2,2,320,128]{3,2,1,0:T(8,128)(2,1)S(1)}, f32[64,128]{1,0:T(8,128)S(1)}, f32[8,128]{1,0:T(8,128)S(1)}) custom-call(bf16[4,2,320,128]{3,2,1,0:T(8,128)(2,1)} %features_hbm.1, f32[1,128]{1,0:T(1,128)} %bitcast.30, f32[1,128]{1,0:T(1,128)} %bitcast.31, f32[1,128]{1,0:T(1,128)} %bitcast.32, f32[1,128]{1,0:T(1,128)} %bitcast.33, ...), custom_call_target="tpu_custom_call" | custom-call | tf_op jit(solution)/shard_map/moments/pallas_call | solution.py:325
  10.3 1.9 %collective-permute-start.2 = (bf16[2,2,320,128]{3,2,1,0:T(8,128)(2,1)S(1)}, bf16[2,2,320,128]{3,2,1,0:T(8,128)(2,1)S(1)}, u32[]{:S(2)}, u32[]{:S(2)}) collective-permute-start(bf16[2,2,320,128]{3,2,1,0:T(8,128)(2,1)S(1)} %get-tuple-element.11), channel_id=1, source_target_pairs={{1,32},{2,33},{3,34},{4,35},{5,36},{6,37},{7,38},{8,39},{9,40},{10... | collective-permute-start | bytes 983048 | tf_op jit(solution)/shard_map/ppermute | solution.py:276
  12.2 4.0 %collective-permute-start.1 = (bf16[2,2,320,128]{3,2,1,0:T(8,128)(2,1)S(1)}, bf16[2,2,320,128]{3,2,1,0:T(8,128)(2,1)S(1)}, u32[]{:S(2)}, u32[]{:S(2)}) collective-permute-start(bf16[2,2,320,128]{3,2,1,0:T(8,128)(2,1)S(1)} %get-tuple-element.11), channel_id=1, source_target_pairs={{0,32},{1,33},{2,34},{3,35},{4,36},{5,37},{6,38},{7,39},{8,40},{9,... | collective-permute-start | bytes 983048 | tf_op jit(solution)/shard_map/ppermute | solution.py:276
  16.2 15.3 %all_to_all.20 = f32[64,1,128]{2,1,0:T(1,128)S(1)} all-to-all(f32[64,1,128]{2,1,0:T(1,128)S(1)} %bitcast.24), channel_id=1, replica_groups=mesh['y'=4,'c'=2,'z'=8,'x'=4] {'y','c','z'}, dimensions={0} | all-to-all | bytes 65536 | tf_op jit(solution)/shard_map/all_to_all | solution.py:292
  31.5 0.3 relay.2
  31.8 7.1 %all_to_all.21 = f32[4,1,128]{2,1,0:T(1,128)S(1)} all-to-all(f32[4,1,128]{2,1,0:T(1,128)S(1)} %bitcast.29), channel_id=1, replica_groups=mesh['y'=4,'c'=2,'z'=8,'x'=4] {'x'}, dimensions={0} | all-to-all | bytes 4096 | tf_op jit(solution)/shard_map/all_to_all | solution.py:292
  39.0 0.0 collective-permute-done.2.diagonal_ref
  39.0 0.0 collective-permute-done.1.back_ref
  39.0 0.0 collective-permute-done.rows_ref
  39.0 0.0 copy-done
  39.0 4.6 %first_conv.1 = (bf16[4,2,320,128]{3,2,1,0:T(8,128)(2,1)S(1)}, bf16[2,2,320,128]{3,2,1,0:T(8,128)(2,1)S(1)}, f32[32,128]{1,0:T(8,128)S(1)}) custom-call(bf16[4,2,320,128]{3,2,1,0:T(8,128)(2,1)S(1)} %copy-done, bf16[4,2,320,128]{3,2,1,0:T(8,128)(2,1)S(1)} %collective-permute-done.rows_ref, bf16[2,2,320,128]{3,2,1,0:T(8,128)(2,1)S(1)} %collective-permute-done.1.back_ref, ...), custom_call_target="tpu_custom_call" | custom-call | tf_op jit(solution)/shard_map/first_conv/pallas_call | solution.py:340
  43.6 0.4 collective-permute-start.3
  44.0 5.6 %collective-permute-start.5 = (bf16[2,2,320,128]{3,2,1,0:T(8,128)(2,1)S(1)}, bf16[2,2,320,128]{3,2,1,0:T(8,128)(2,1)S(1)}, u32[]{:S(2)}, u32[]{:S(2)}) collective-permute-start(bf16[2,2,320,128]{3,2,1,0:T(8,128)(2,1)S(1)} %get-tuple-element.15), channel_id=1, source_target_pairs={{1,32},{2,33},{3,34},{4,35},{5,36},{6,37},{7,38},{8,39},{9,40},{10... | collective-permute-start | bytes 983048 | tf_op jit(solution)/shard_map/ppermute | solution.py:276
  49.6 3.4 %collective-permute-start.4 = (bf16[2,2,320,128]{3,2,1,0:T(8,128)(2,1)S(1)}, bf16[2,2,320,128]{3,2,1,0:T(8,128)(2,1)S(1)}, u32[]{:S(2)}, u32[]{:S(2)}) collective-permute-start(bf16[2,2,320,128]{3,2,1,0:T(8,128)(2,1)S(1)} %get-tuple-element.15), channel_id=1, source_target_pairs={{0,32},{1,33},{2,34},{3,35},{4,36},{5,37},{6,38},{7,39},{8,40},{9,... | collective-permute-start | bytes 983048 | tf_op jit(solution)/shard_map/ppermute | solution.py:276
  53.0 12.2 %all_to_all.22 = f32[32,1,128]{2,1,0:T(1,128)S(1)} all-to-all(f32[32,1,128]{2,1,0:T(1,128)S(1)} %bitcast.26), channel_id=1, replica_groups=mesh['y'=4,'c'=2,'z'=8,'x'=4] {'y','z'}, dimensions={0} | all-to-all | bytes 32768 | tf_op jit(solution)/shard_map/all_to_all | solution.py:292
  65.2 0.3 relay.3
  65.5 10.2 %all_to_all.23 = f32[8,1,128]{2,1,0:T(1,128)S(1)} all-to-all(f32[8,1,128]{2,1,0:T(1,128)S(1)} %bitcast.25), channel_id=1, replica_groups=mesh['y'=4,'c'=2,'z'=8,'x'=4] {'c','x'}, dimensions={0} | all-to-all | bytes 8192 | tf_op jit(solution)/shard_map/all_to_all | solution.py:292
  75.7 0.0 collective-permute-done.5.diagonal_ref
  75.7 0.0 collective-permute-done.4.back_ref
  75.7 0.0 collective-permute-done.3.rows_ref
  75.7 5.0 %second_conv.1 = bf16[4,2,320,128]{3,2,1,0:T(8,128)(2,1)} custom-call(bf16[4,2,320,128]{3,2,1,0:T(8,128)(2,1)S(1)} %get-tuple-element.14.own_ref, bf16[4,2,320,128]{3,2,1,0:T(8,128)(2,1)S(1)} %collective-permute-done.3.rows_ref, bf16[2,2,320,128]{3,2,1,0:T(8,128)(2,1)S(1)} %collective-permute-done.4.back_ref, ...), custom_call_target="tpu_custom_call" | custom-call | tf_op jit(solution)/shard_map/second_conv/pallas_call | solution.py:352
Async XLA Ops:
  0.0 39.0 %copy-start = (bf16[4,2,320,128]{3,2,1,0:T(8,128)(2,1)S(1)}, bf16[4,2,320,128]{3,2,1,0:T(8,128)(2,1)}, u32[]{:S(2)}) copy-start(bf16[4,2,320,128]{3,2,1,0:T(8,128)(2,1)} %features_hbm.1) | copy-start | bytes 1966084
  0.0 39.0 %collective-permute-start = (bf16[4,2,320,128]{3,2,1,0:T(8,128)(2,1)}, bf16[4,2,320,128]{3,2,1,0:T(8,128)(2,1)S(1)}, u32[]{:S(2)}, u32[]{:S(2)}) collective-permute-start(bf16[4,2,320,128]{3,2,1,0:T(8,128)(2,1)} %features_hbm.1), channel_id=1, source_target_pairs={{31,0},{0,1},{1,2},{2,3},{3,4},{4,5},{5,6},{6,7},{7,8},{8,9},{9,10... | collective-permute-start | bytes 1966088 | tf_op jit(solution)/shard_map/ppermute | solution.py:276
  10.3 28.7 %collective-permute-start.2 = (bf16[2,2,320,128]{3,2,1,0:T(8,128)(2,1)S(1)}, bf16[2,2,320,128]{3,2,1,0:T(8,128)(2,1)S(1)}, u32[]{:S(2)}, u32[]{:S(2)}) collective-permute-start(bf16[2,2,320,128]{3,2,1,0:T(8,128)(2,1)S(1)} %get-tuple-element.11), channel_id=1, source_target_pairs={{1,32},{2,33},{3,34},{4,35},{5,36},{6,37},{7,38},{8,39},{9,40},{10... | collective-permute-start | bytes 983048 | tf_op jit(solution)/shard_map/ppermute | solution.py:276
  12.2 26.8 %collective-permute-start.1 = (bf16[2,2,320,128]{3,2,1,0:T(8,128)(2,1)S(1)}, bf16[2,2,320,128]{3,2,1,0:T(8,128)(2,1)S(1)}, u32[]{:S(2)}, u32[]{:S(2)}) collective-permute-start(bf16[2,2,320,128]{3,2,1,0:T(8,128)(2,1)S(1)} %get-tuple-element.11), channel_id=1, source_target_pairs={{0,32},{1,33},{2,34},{3,35},{4,36},{5,37},{6,38},{7,39},{8,40},{9,... | collective-permute-start | bytes 983048 | tf_op jit(solution)/shard_map/ppermute | solution.py:276
  43.6 32.1 %collective-permute-start.3 = (bf16[4,2,320,128]{3,2,1,0:T(8,128)(2,1)S(1)}, bf16[4,2,320,128]{3,2,1,0:T(8,128)(2,1)S(1)}, u32[]{:S(2)}, u32[]{:S(2)}) collective-permute-start(bf16[4,2,320,128]{3,2,1,0:T(8,128)(2,1)S(1)} %get-tuple-element.14.own_ref), channel_id=1, source_target_pairs={{1,0},{2,1},{3,2},{4,3},{5,4},{6,5},{7,6},{8,7},{9,8},{10,9},{11,1... | collective-permute-start | bytes 1966088 | tf_op jit(solution)/shard_map/ppermute | solution.py:276
  44.0 31.7 %collective-permute-start.5 = (bf16[2,2,320,128]{3,2,1,0:T(8,128)(2,1)S(1)}, bf16[2,2,320,128]{3,2,1,0:T(8,128)(2,1)S(1)}, u32[]{:S(2)}, u32[]{:S(2)}) collective-permute-start(bf16[2,2,320,128]{3,2,1,0:T(8,128)(2,1)S(1)} %get-tuple-element.15), channel_id=1, source_target_pairs={{1,32},{2,33},{3,34},{4,35},{5,36},{6,37},{7,38},{8,39},{9,40},{10... | collective-permute-start | bytes 983048 | tf_op jit(solution)/shard_map/ppermute | solution.py:276
  49.6 26.1 %collective-permute-start.4 = (bf16[2,2,320,128]{3,2,1,0:T(8,128)(2,1)S(1)}, bf16[2,2,320,128]{3,2,1,0:T(8,128)(2,1)S(1)}, u32[]{:S(2)}, u32[]{:S(2)}) collective-permute-start(bf16[2,2,320,128]{3,2,1,0:T(8,128)(2,1)S(1)} %get-tuple-element.15), channel_id=1, source_target_pairs={{0,32},{1,33},{2,34},{3,35},{4,36},{5,37},{6,38},{7,39},{8,40},{9,... | collective-permute-start | bytes 983048 | tf_op jit(solution)/shard_map/ppermute | solution.py:276
where the time goes:
time: 81.1 us; the launch traced here: 80.7 us
  blocking collectives  44.8 us (55%)
  starting transfers between devices  23.9 us (29%)
  Pallas kernels  11.9 us (15%)
    all_to_all x4, blocking collectives, exchanged(): lax.all_to_all(copies.reshape(count, 1, C), axes, split_axis=0, concat_ax...  44.8 us
    ppermute x6, starting transfers between devices, sent(): return lax.ppermute(block, EVERY, route)  23.9 us
    pallas_call x1, Pallas kernels, body(): pl.pallas_call(functools.partial(second_conv_kernel, devices, last_row),...  5.01 us
    pallas_call x1, Pallas kernels, body(): pl.pallas_call(functools.partial(first_conv_kernel, devices, last_row), o...  4.62 us
    pallas_call x1, Pallas kernels, body(): pl.pallas_call(moments_kernel, out_shape=(two, copies_one, jax.ShapeDtype...  1.69 us
  transfers between devices with their start and end apart: 6, of which 0 were waited for; matrix products, arithmetic and copies ran while one was open for 0% of the time, Pallas kernels for 3%

commit v1 on v0

--- a/solution.py
+++ b/solution.py
@@ -13,8 +13,8 @@
 TM = ("y", "c")
 ROWS = ("z", "x")
 EVERY = TM + ROWS
-STAGES_ONE = (("y", "c", "z"), ("x",))
-STAGES_TWO = (("y", "z"), ("c", "x"))
+FAR = ("y", "z")
+NEAR = ("c", "x")
 EPS = 1e-06
 MIB = 1 << 20
 VMEM = pl.BlockSpec(memory_space=pltpu.VMEM)
@@ -40,7 +40,7 @@
 
 
 def column_total(rows):
-    total = rows if rows.shape[0] < 8 else jnp.sum(rows.reshape(rows.shape[0] // 8, 8, C), axis=0)
+    total = jnp.sum(rows.reshape(rows.shape[0] // 8, 8, C), axis=0)
     return jnp.broadcast_to(jnp.sum(total, axis=0, keepdims=True), (8, C))
 
 
@@ -293,28 +293,25 @@
     return received.reshape(count, C)
 
 
-def everywhere(copies, tile_cells, stages):
-    far, near = stages
-    sums = exchanged(copies, far)
+def everywhere(copies, tile_cells):
+    sums = exchanged(copies, FAR)
     copies = pl.pallas_call(
         functools.partial(relay_kernel, tile_cells * GROUP),
-        out_shape=jax.ShapeDtypeStruct((lax.axis_size(near), C), jnp.float32),
+        out_shape=jax.ShapeDtypeStruct((lax.axis_size(NEAR), C), jnp.float32),
         in_specs=[VMEM],
         out_specs=VMEM,
         name="relay",
         cost_estimate=pl.CostEstimate(flops=0, bytes_accessed=1 << 24, transcendentals=0),
         compiler_params=pltpu.CompilerParams(vmem_limit_bytes=4 * MIB),
     )(sums)
-    return exchanged(copies, near)
+    return exchanged(copies, NEAR)
 
 
 def body(features, gain_one, shift_one, weight_one, bias_one, gain_two, shift_two, weight_two, bias_two):
     frames, rows, width, _ = features.shape
     devices = lax.axis_size(EVERY)
     tile_cells = frames * rows * width
-    copies_one, copies_two = (
-        jax.ShapeDtypeStruct((lax.axis_size(stages[0]), C), jnp.float32) for stages in (STAGES_ONE, STAGES_TWO)
-    )
+    copies = jax.ShapeDtypeStruct((lax.axis_size(FAR), C), jnp.float32)
     tile = jax.ShapeDtypeStruct(features.shape, jnp.bfloat16)
     two = jax.ShapeDtypeStruct((2, rows, width, C), jnp.bfloat16)
     last_row = lax.axis_size(ROWS) - 1
@@ -324,7 +321,7 @@
 
     last, sums, vectors = pl.pallas_call(
         moments_kernel,
-        out_shape=(two, copies_one, jax.ShapeDtypeStruct((8, C), jnp.float32)),
+        out_shape=(two, copies, jax.ShapeDtypeStruct((8, C), jnp.float32)),
         in_specs=[HBM] * 7,
         out_specs=(VMEM,) * 3,
         scratch_shapes=[
@@ -336,10 +333,10 @@
         compiler_params=pltpu.CompilerParams(vmem_limit_bytes=4 * MIB),
     )(*(in_hbm(v) for v in (features, *vectors)))
     around = neighbours(features, last, (-1, 1))
-    sums = everywhere(sums, tile_cells, STAGES_ONE)
+    sums = everywhere(sums, tile_cells)
     hidden, last, sums_two = pl.pallas_call(
         functools.partial(first_conv_kernel, devices, last_row),
-        out_shape=(tile, two, copies_two),
+        out_shape=(tile, two, copies),
         in_specs=[VMEM] * 6 + [HBM],
         out_specs=(VMEM,) * 3,
         scratch_shapes=[held, pltpu.VMEM(weight_one.shape, weight_one.dtype), pltpu.SemaphoreType.DMA],
@@ -348,7 +345,7 @@
     )(features, *around, sums, vectors, in_hbm(weight_one))
 
     around = neighbours(hidden, last, (1, -1))
-    sums_two = everywhere(sums_two, tile_cells, STAGES_TWO)
+    sums_two = everywhere(sums_two, tile_cells)
     return pl.pallas_call(
         functools.partial(second_conv_kernel, devices, last_row),
         out_shape=tile,

time: 81.1 us -> 80.8 us (level)
  no operation moved by 1% of the time
where the time goes in v1:
time: 80.8 us; the launch traced here: 80.4 us
  blocking collectives  44.6 us (55%)
  starting transfers between devices  23.8 us (29%)
  Pallas kernels  11.9 us (15%)
    all_to_all x4, blocking collectives, exchanged(): lax.all_to_all(copies.reshape(count, 1, C), axes, split_axis=0, concat_ax...  44.6 us
    ppermute x6, starting transfers between devices, sent(): return lax.ppermute(block, EVERY, route)  23.8 us
    pallas_call x1, Pallas kernels, body(): pl.pallas_call(functools.partial(second_conv_kernel, devices, last_row),...  5.01 us
    pallas_call x1, Pallas kernels, body(): pl.pallas_call(functools.partial(first_conv_kernel, devices, last_row), o...  4.62 us
    pallas_call x1, Pallas kernels, body(): pl.pallas_call(moments_kernel, out_shape=(two, copies, jax.ShapeDtypeStru...  1.69 us
  transfers between devices with their start and end apart: 6, of which 0 were waited for; matrix products, arithmetic and copies ran while one was open for 0% of the time, Pallas kernels for 3%

profile of v1, /device:TPU:1, one launch (start us, length us, event | category | flops | bytes accessed | tf_op | source)
XLA Modules:
  0.0 80.4 jit_solution(11584391661314618501)
XLA Ops:
  0.0 0.0 copy-start
  0.0 8.6 %collective-permute-start = (bf16[4,2,320,128]{3,2,1,0:T(8,128)(2,1)}, bf16[4,2,320,128]{3,2,1,0:T(8,128)(2,1)S(1)}, u32[]{:S(2)}, u32[]{:S(2)}) collective-permute-start(bf16[4,2,320,128]{3,2,1,0:T(8,128)(2,1)} %features_hbm.1), channel_id=1, source_target_pairs={{31,0},{0,1},{1,2},{2,3},{3,4},{4,5},{5,6},{6,7},{7,8},{8,9},{9,10... | collective-permute-start | bytes 1966088 | tf_op jit(solution)/shard_map/ppermute | solution.py:276
  8.6 1.7 %moments.1 = (bf16[2,2,320,128]{3,2,1,0:T(8,128)(2,1)S(1)}, f32[32,128]{1,0:T(8,128)S(1)}, f32[8,128]{1,0:T(8,128)S(1)}) custom-call(bf16[4,2,320,128]{3,2,1,0:T(8,128)(2,1)} %features_hbm.1, f32[1,128]{1,0:T(1,128)} %bitcast.30, f32[1,128]{1,0:T(1,128)} %bitcast.31, f32[1,128]{1,0:T(1,128)} %bitcast.32, f32[1,128]{1,0:T(1,128)} %bitcast.33, ...), custom_call_target="tpu_custom_call" | custom-call | tf_op jit(solution)/shard_map/moments/pallas_call | solution.py:322
  10.3 1.9 %collective-permute-start.2 = (bf16[2,2,320,128]{3,2,1,0:T(8,128)(2,1)S(1)}, bf16[2,2,320,128]{3,2,1,0:T(8,128)(2,1)S(1)}, u32[]{:S(2)}, u32[]{:S(2)}) collective-permute-start(bf16[2,2,320,128]{3,2,1,0:T(8,128)(2,1)S(1)} %get-tuple-element.11), channel_id=1, source_target_pairs={{1,32},{2,33},{3,34},{4,35},{5,36},{6,37},{7,38},{8,39},{9,40},{10... | collective-permute-start | bytes 983048 | tf_op jit(solution)/shard_map/ppermute | solution.py:276
  12.2 4.0 %collective-permute-start.1 = (bf16[2,2,320,128]{3,2,1,0:T(8,128)(2,1)S(1)}, bf16[2,2,320,128]{3,2,1,0:T(8,128)(2,1)S(1)}, u32[]{:S(2)}, u32[]{:S(2)}) collective-permute-start(bf16[2,2,320,128]{3,2,1,0:T(8,128)(2,1)S(1)} %get-tuple-element.11), channel_id=1, source_target_pairs={{0,32},{1,33},{2,34},{3,35},{4,36},{5,37},{6,38},{7,39},{8,40},{9,... | collective-permute-start | bytes 983048 | tf_op jit(solution)/shard_map/ppermute | solution.py:276
  16.2 14.1 %all_to_all.20 = f32[32,1,128]{2,1,0:T(1,128)S(1)} all-to-all(f32[32,1,128]{2,1,0:T(1,128)S(1)} %bitcast.28), channel_id=1, replica_groups=mesh['y'=4,'c'=2,'z'=8,'x'=4] {'y','z'}, dimensions={0} | all-to-all | bytes 32768 | tf_op jit(solution)/shard_map/all_to_all | solution.py:292
  30.3 0.3 relay.2
  30.6 9.5 %all_to_all.21 = f32[8,1,128]{2,1,0:T(1,128)S(1)} all-to-all(f32[8,1,128]{2,1,0:T(1,128)S(1)} %bitcast.25), channel_id=1, replica_groups=mesh['y'=4,'c'=2,'z'=8,'x'=4] {'c','x'}, dimensions={0} | all-to-all | bytes 8192 | tf_op jit(solution)/shard_map/all_to_all | solution.py:292
  40.1 0.0 collective-permute-done.2.diagonal_ref
  40.1 0.0 collective-permute-done.1.back_ref
  40.1 0.0 collective-permute-done.rows_ref
  40.1 0.0 copy-done
  40.1 4.6 %first_conv.1 = (bf16[4,2,320,128]{3,2,1,0:T(8,128)(2,1)S(1)}, bf16[2,2,320,128]{3,2,1,0:T(8,128)(2,1)S(1)}, f32[32,128]{1,0:T(8,128)S(1)}) custom-call(bf16[4,2,320,128]{3,2,1,0:T(8,128)(2,1)S(1)} %copy-done, bf16[4,2,320,128]{3,2,1,0:T(8,128)(2,1)S(1)} %collective-permute-done.rows_ref, bf16[2,2,320,128]{3,2,1,0:T(8,128)(2,1)S(1)} %collective-permute-done.1.back_ref, ...), custom_call_target="tpu_custom_call" | custom-call | tf_op jit(solution)/shard_map/first_conv/pallas_call | solution.py:337
  44.8 0.4 collective-permute-start.3
  45.1 4.0 %collective-permute-start.5 = (bf16[2,2,320,128]{3,2,1,0:T(8,128)(2,1)S(1)}, bf16[2,2,320,128]{3,2,1,0:T(8,128)(2,1)S(1)}, u32[]{:S(2)}, u32[]{:S(2)}) collective-permute-start(bf16[2,2,320,128]{3,2,1,0:T(8,128)(2,1)S(1)} %get-tuple-element.15), channel_id=1, source_target_pairs={{1,32},{2,33},{3,34},{4,35},{5,36},{6,37},{7,38},{8,39},{9,40},{10... | collective-permute-start | bytes 983048 | tf_op jit(solution)/shard_map/ppermute | solution.py:276
  49.1 4.9 %collective-permute-start.4 = (bf16[2,2,320,128]{3,2,1,0:T(8,128)(2,1)S(1)}, bf16[2,2,320,128]{3,2,1,0:T(8,128)(2,1)S(1)}, u32[]{:S(2)}, u32[]{:S(2)}) collective-permute-start(bf16[2,2,320,128]{3,2,1,0:T(8,128)(2,1)S(1)} %get-tuple-element.15), channel_id=1, source_target_pairs={{0,32},{1,33},{2,34},{3,35},{4,36},{5,37},{6,38},{7,39},{8,40},{9,... | collective-permute-start | bytes 983048 | tf_op jit(solution)/shard_map/ppermute | solution.py:276
  54.1 12.0 %all_to_all.22 = f32[32,1,128]{2,1,0:T(1,128)S(1)} all-to-all(f32[32,1,128]{2,1,0:T(1,128)S(1)} %bitcast.27), channel_id=1, replica_groups=mesh['y'=4,'c'=2,'z'=8,'x'=4] {'y','z'}, dimensions={0} | all-to-all | bytes 32768 | tf_op jit(solution)/shard_map/all_to_all | solution.py:292
  66.0 0.3 relay.3
  66.3 9.1 %all_to_all.23 = f32[8,1,128]{2,1,0:T(1,128)S(1)} all-to-all(f32[8,1,128]{2,1,0:T(1,128)S(1)} %bitcast.26), channel_id=1, replica_groups=mesh['y'=4,'c'=2,'z'=8,'x'=4] {'c','x'}, dimensions={0} | all-to-all | bytes 8192 | tf_op jit(solution)/shard_map/all_to_all | solution.py:292
  75.4 0.0 collective-permute-done.5.diagonal_ref
  75.4 0.0 collective-permute-done.4.back_ref
  75.4 0.0 collective-permute-done.3.rows_ref
  75.4 5.0 %second_conv.1 = bf16[4,2,320,128]{3,2,1,0:T(8,128)(2,1)} custom-call(bf16[4,2,320,128]{3,2,1,0:T(8,128)(2,1)S(1)} %get-tuple-element.14.own_ref, bf16[4,2,320,128]{3,2,1,0:T(8,128)(2,1)S(1)} %collective-permute-done.3.rows_ref, bf16[2,2,320,128]{3,2,1,0:T(8,128)(2,1)S(1)} %collective-permute-done.4.back_ref, ...), custom_call_target="tpu_custom_call" | custom-call | tf_op jit(solution)/shard_map/second_conv/pallas_call | solution.py:349
Async XLA Ops:
  0.0 40.1 %copy-start = (bf16[4,2,320,128]{3,2,1,0:T(8,128)(2,1)S(1)}, bf16[4,2,320,128]{3,2,1,0:T(8,128)(2,1)}, u32[]{:S(2)}) copy-start(bf16[4,2,320,128]{3,2,1,0:T(8,128)(2,1)} %features_hbm.1) | copy-start | bytes 1966084
  0.0 40.1 %collective-permute-start = (bf16[4,2,320,128]{3,2,1,0:T(8,128)(2,1)}, bf16[4,2,320,128]{3,2,1,0:T(8,128)(2,1)S(1)}, u32[]{:S(2)}, u32[]{:S(2)}) collective-permute-start(bf16[4,2,320,128]{3,2,1,0:T(8,128)(2,1)} %features_hbm.1), channel_id=1, source_target_pairs={{31,0},{0,1},{1,2},{2,3},{3,4},{4,5},{5,6},{6,7},{7,8},{8,9},{9,10... | collective-permute-start | bytes 1966088 | tf_op jit(solution)/shard_map/ppermute | solution.py:276
  10.3 29.8 %collective-permute-start.2 = (bf16[2,2,320,128]{3,2,1,0:T(8,128)(2,1)S(1)}, bf16[2,2,320,128]{3,2,1,0:T(8,128)(2,1)S(1)}, u32[]{:S(2)}, u32[]{:S(2)}) collective-permute-start(bf16[2,2,320,128]{3,2,1,0:T(8,128)(2,1)S(1)} %get-tuple-element.11), channel_id=1, source_target_pairs={{1,32},{2,33},{3,34},{4,35},{5,36},{6,37},{7,38},{8,39},{9,40},{10... | collective-permute-start | bytes 983048 | tf_op jit(solution)/shard_map/ppermute | solution.py:276
  12.2 27.9 %collective-permute-start.1 = (bf16[2,2,320,128]{3,2,1,0:T(8,128)(2,1)S(1)}, bf16[2,2,320,128]{3,2,1,0:T(8,128)(2,1)S(1)}, u32[]{:S(2)}, u32[]{:S(2)}) collective-permute-start(bf16[2,2,320,128]{3,2,1,0:T(8,128)(2,1)S(1)} %get-tuple-element.11), channel_id=1, source_target_pairs={{0,32},{1,33},{2,34},{3,35},{4,36},{5,37},{6,38},{7,39},{8,40},{9,... | collective-permute-start | bytes 983048 | tf_op jit(solution)/shard_map/ppermute | solution.py:276
  44.8 30.6 %collective-permute-start.3 = (bf16[4,2,320,128]{3,2,1,0:T(8,128)(2,1)S(1)}, bf16[4,2,320,128]{3,2,1,0:T(8,128)(2,1)S(1)}, u32[]{:S(2)}, u32[]{:S(2)}) collective-permute-start(bf16[4,2,320,128]{3,2,1,0:T(8,128)(2,1)S(1)} %get-tuple-element.14.own_ref), channel_id=1, source_target_pairs={{1,0},{2,1},{3,2},{4,3},{5,4},{6,5},{7,6},{8,7},{9,8},{10,9},{11,1... | collective-permute-start | bytes 1966088 | tf_op jit(solution)/shard_map/ppermute | solution.py:276
  45.1 30.3 %collective-permute-start.5 = (bf16[2,2,320,128]{3,2,1,0:T(8,128)(2,1)S(1)}, bf16[2,2,320,128]{3,2,1,0:T(8,128)(2,1)S(1)}, u32[]{:S(2)}, u32[]{:S(2)}) collective-permute-start(bf16[2,2,320,128]{3,2,1,0:T(8,128)(2,1)S(1)} %get-tuple-element.15), channel_id=1, source_target_pairs={{1,32},{2,33},{3,34},{4,35},{5,36},{6,37},{7,38},{8,39},{9,40},{10... | collective-permute-start | bytes 983048 | tf_op jit(solution)/shard_map/ppermute | solution.py:276
  49.1 26.3 %collective-permute-start.4 = (bf16[2,2,320,128]{3,2,1,0:T(8,128)(2,1)S(1)}, bf16[2,2,320,128]{3,2,1,0:T(8,128)(2,1)S(1)}, u32[]{:S(2)}, u32[]{:S(2)}) collective-permute-start(bf16[2,2,320,128]{3,2,1,0:T(8,128)(2,1)S(1)} %get-tuple-element.15), channel_id=1, source_target_pairs={{0,32},{1,33},{2,34},{3,35},{4,36},{5,37},{6,38},{7,39},{8,40},{9,... | collective-permute-start | bytes 983048 | tf_op jit(solution)/shard_map/ppermute | solution.py:276
